TPU v7x, 32 devices: a whole 2x2x4 slice. The times are simulated.
32 devices in a mesh: lat: 4 (over y, x), lon: 8 (over z, core).
Axes of the slice: x: 2, y: 2, z: 4, core: 2. Of those that a mesh axis runs over, the one named last changes fastest.
Arguments:
- queries: bfloat16 [64, 64, 768], P('lat', 'lon'), may hold values from -8 to 8
- key_vectors: bfloat16 [64, 64, 768], P('lat', 'lon'), may hold values from -8 to 8
- value_vectors: bfloat16 [64, 64, 768], P('lat', 'lon'), may hold values from -12 to 12
- upstream: bfloat16 [64, 64, 768], P('lat', 'lon'), may hold values from -6 to 6
- w_out: bfloat16 [768, 768], replicated, may hold values from -0.21875 to 0.21875
- neighbours: int32 [8, 8, 4], replicated, may hold values from 0 to 63, as said below
- counts: int32 [8, 8], replicated, may hold values from 2 to 4, as said below
Outputs:
- mixed_out: bfloat16 [64, 64, 768], P('lat', 'lon')
- q_grad: bfloat16 [64, 64, 768], P('lat', 'lon')
- k_grad: bfloat16 [64, 64, 768], P('lat', 'lon')
- v_grad: bfloat16 [64, 64, 768], P('lat', 'lon')
- w_grad: float32 [768, 768], replicated
Inputs may be any that keep to these rules, and one draw needn't show every extreme that they name: `neighbours`: entry s of block (i, j) names a block i2 * 8 + j2 with i2 within one of i and j2 within one of j around the longitude circle; slot 0 names the block itself, the entries of slots below counts[i, j] are distinct, and the slots at or beyond counts[i, j] name the block itself. `counts`: every block outside the first and the last row of blocks has 4.
All inputs are finite; a program needn't handle non-finite values.
Results may differ from a plain program's by a relative error of at most 0.03.
Values may be sent and summed in bfloat16 or wider, within the bound.
No kernel may reach another device: no remote copies, remote signals or barrier semaphores. Data moves between devices by JAX's collectives and lax.ppermute only.
A program may use at most 64 MiB of HBM per device.

v0:
```python
import math
import jax
import jax.numpy as jnp
from jax import lax
from jax.sharding import PartitionSpec as P

HEADS = 12
HEAD_DIM = 64
BLK = 8
SLOTS = 4


def padded_2(value, sides, width):
    for axis, dim in sides:
        peers, length = (lax.axis_size(axis), value.shape[dim])
        up = [(i, (i + 1) % peers) for i in range(peers)]
        down = [(j, i) for i, j in up]
        last = lax.slice_in_dim(value, length - width, length, axis=dim)
        leading = lax.slice_in_dim(value, 0, width, axis=dim)
        before = lax.ppermute(last, axis, up)
        after = lax.ppermute(leading, axis, down)
        value = jnp.concatenate([before, value, after], axis=dim)
    return value


def to_blocks(token_grid):
    lat_rows, lon_cols, feat_width = token_grid.shape
    block_tiles = token_grid.reshape(
        lat_rows // BLK, BLK, lon_cols // BLK, BLK, feat_width
    ).transpose(0, 2, 1, 3, 4)
    return block_tiles.reshape(lat_rows // BLK * (lon_cols // BLK), BLK * BLK, feat_width)


def from_blocks(block_tiles, lat_blocks, lon_blocks):
    feat_width = block_tiles.shape[-1]
    token_grid = block_tiles.reshape(lat_blocks, lon_blocks, BLK, BLK, feat_width).transpose(
        0, 2, 1, 3, 4
    )
    return token_grid.reshape(lat_blocks * BLK, lon_blocks * BLK, feat_width)


def split_heads(block_tiles):
    return block_tiles.reshape(block_tiles.shape[0], block_tiles.shape[1], HEADS, HEAD_DIM)


def slot_places(
    neighbours,
    counts,
    first_lat,
    first_lon,
    grid_rows,
    grid_cols,
    anchor_lat,
    anchor_lon,
    pad_rows,
    pad_cols,
):
    total_lat = neighbours.shape[0]
    total_lon = neighbours.shape[1]
    block_lat = first_lat + jnp.arange(grid_rows, dtype=jnp.int32)
    block_lon = (first_lon + jnp.arange(grid_cols, dtype=jnp.int32)) % total_lon
    inside = (block_lat >= 0) & (block_lat < total_lat)
    safe_lat = jnp.clip(block_lat, 0, total_lat - 1)
    slot_table = jnp.take(jnp.take(neighbours, safe_lat, axis=0), block_lon, axis=1)
    slot_limit = jnp.take(jnp.take(counts, safe_lat, axis=0), block_lon, axis=1)
    slot_ids = jnp.arange(SLOTS, dtype=jnp.int32)
    rel_lat = slot_table // total_lon - anchor_lat
    rel_lon = (slot_table % total_lon - anchor_lon) % total_lon
    usable = (slot_ids[None, None, :] < slot_limit[:, :, None]) & inside[:, None, None]
    usable = usable & (rel_lat >= 0) & (rel_lat < pad_rows) & (rel_lon < pad_cols)
    key_place = jnp.where(usable, rel_lat * pad_cols + rel_lon, 0)
    return (
        key_place.reshape(grid_rows * grid_cols, SLOTS),
        usable.reshape(grid_rows * grid_cols, SLOTS),
    )


def gather_sets(padded_tiles, key_place):
    picked = jnp.take(padded_tiles, key_place.reshape(-1), axis=0)
    return picked.reshape(key_place.shape[0], SLOTS * BLK * BLK, padded_tiles.shape[-1])


def masked_scores(query_tiles, key_sets, key_valid):
    raw = jnp.einsum(
        "nqhd,nkhd->nhqk",
        split_heads(query_tiles),
        split_heads(key_sets),
        preferred_element_type=jnp.float32,
    )
    raw = raw * (1.0 / math.sqrt(HEAD_DIM))
    return jnp.where(key_valid[:, None, None, :], raw, -jnp.inf)


def forward_core(query_tiles, key_sets, value_sets, key_valid):
    masked = masked_scores(query_tiles, key_sets, key_valid)
    row_top = jnp.max(masked, axis=-1, keepdims=True)
    exp_total = jnp.sum(jnp.exp(masked - row_top), axis=-1, keepdims=True)
    log_total = row_top + jnp.log(exp_total)
    attn_probs = jnp.exp(masked - log_total)
    probs_low = attn_probs.astype(jnp.bfloat16)
    mixed_heads = jnp.einsum(
        "nhqk,nkhd->nqhd", probs_low, split_heads(value_sets), preferred_element_type=jnp.float32
    )
    attended = mixed_heads.astype(jnp.bfloat16).reshape(query_tiles.shape)
    return (attended, attn_probs, probs_low, log_total[..., 0])


def head_delta(d_att, attended):
    product = d_att.astype(jnp.float32) * attended.astype(jnp.float32)
    return jnp.sum(split_heads(product), axis=-1).transpose(0, 2, 1)


def backward_scores(attn_probs, d_att, row_delta, value_sets):
    dprobs = jnp.einsum(
        "nqhd,nkhd->nhqk",
        split_heads(d_att),
        split_heads(value_sets),
        preferred_element_type=jnp.float32,
    )
    return (attn_probs * (dprobs - row_delta[..., None]) * (1.0 / math.sqrt(HEAD_DIM))).astype(
        jnp.bfloat16
    )


def grad_queries(dscores, key_sets):
    summed = jnp.einsum(
        "nhqk,nkhd->nqhd", dscores, split_heads(key_sets), preferred_element_type=jnp.float32
    )
    return summed.astype(jnp.bfloat16).reshape(summed.shape[0], summed.shape[1], -1)


def contract_keys(weights_low, block_tiles):
    summed = jnp.einsum(
        "nhqk,nqhd->nkhd", weights_low, split_heads(block_tiles), preferred_element_type=jnp.float32
    )
    return summed.reshape(summed.shape[0], summed.shape[1], -1)


def add_into(contrib, key_place, usable, pad_count):
    flat_place = key_place.reshape(-1)
    feat_width = contrib.shape[-1]
    flat_terms = contrib.reshape(flat_place.shape[0], BLK * BLK * feat_width)
    flat_terms = jnp.where(usable.reshape(-1)[:, None], flat_terms, 0.0)
    summed = (
        jnp.zeros((pad_count, BLK * BLK * feat_width), jnp.float32).at[flat_place].add(flat_terms)
    )
    return summed.reshape(pad_count, BLK * BLK, feat_width)


def fold_joint(extended, lat_rows, lon_cols):
    low_lat = lat_rows + 3 * BLK
    low_lon = lon_cols + 3 * BLK
    interior = extended[:, 2 * BLK : 2 * BLK + lat_rows, 2 * BLK : 2 * BLK + lon_cols]
    interior = interior.at[:, :BLK, :].add(extended[:, :BLK, 2 * BLK : 2 * BLK + lon_cols])
    interior = interior.at[:, lat_rows - BLK :, :].add(
        extended[:, low_lat:, 2 * BLK : 2 * BLK + lon_cols]
    )
    interior = interior.at[:, :, :BLK].add(extended[:, 2 * BLK : 2 * BLK + lat_rows, :BLK])
    interior = interior.at[:, :, lon_cols - BLK :].add(
        extended[:, 2 * BLK : 2 * BLK + lat_rows, low_lon:]
    )
    interior = interior.at[:, :BLK, :BLK].add(extended[:, :BLK, :BLK])
    interior = interior.at[:, :BLK, lon_cols - BLK :].add(extended[:, :BLK, low_lon:])
    interior = interior.at[:, lat_rows - BLK :, :BLK].add(extended[:, low_lat:, :BLK])
    return interior.at[:, lat_rows - BLK :, lon_cols - BLK :].add(extended[:, low_lat:, low_lon:])


def on_device(queries, key_vectors, value_vectors, upstream, w_out, neighbours, counts):
    lat_rows, lon_cols, feat_width = queries.shape
    lat_blocks = lat_rows // BLK
    lon_blocks = lon_cols // BLK
    pad_rows = lat_blocks + 2
    pad_cols = lon_blocks + 2
    pad_count = pad_rows * pad_cols
    inner_count = BLK * BLK
    tokens_all = lat_rows * lon_cols * lax.axis_size("lat") * lax.axis_size("lon")
    first_lat = lax.axis_index("lat") * lat_blocks
    first_lon = lax.axis_index("lon") * lon_blocks
    stacked = jnp.stack((key_vectors, value_vectors))
    padded = padded_2(stacked, (("lat", 1), ("lon", 2)), BLK)
    key_tiles = to_blocks(padded[0])
    value_tiles = to_blocks(padded[1])
    own_place, own_usable = slot_places(
        neighbours,
        counts,
        first_lat,
        first_lon,
        lat_blocks,
        lon_blocks,
        first_lat - 1,
        first_lon - 1,
        pad_rows,
        pad_cols,
    )
    query_tiles = to_blocks(queries)
    key_sets = gather_sets(key_tiles, own_place)
    value_sets = gather_sets(value_tiles, own_place)
    key_valid = jnp.repeat(own_usable, inner_count, axis=1)
    attended, attn_probs, probs_low, log_total = forward_core(
        query_tiles, key_sets, value_sets, key_valid
    )
    flat_att = attended.reshape(-1, feat_width)
    mixed_flat = jnp.dot(flat_att, w_out, preferred_element_type=jnp.float32).astype(jnp.bfloat16)
    grad_tiles = to_blocks(upstream)
    flat_grad = grad_tiles.reshape(-1, feat_width)
    local_weight = lax.dot_general(
        flat_att, flat_grad, (((0,), (0,)), ((), ())), preferred_element_type=jnp.float32
    )
    w_grad = lax.psum(local_weight, ("lat", "lon")) / math.sqrt(tokens_all)
    d_att = lax.dot_general(
        flat_grad, w_out, (((1,), (1,)), ((), ())), preferred_element_type=jnp.float32
    )
    d_att = d_att.astype(jnp.bfloat16).reshape(attended.shape)
    row_delta = head_delta(d_att, attended)
    dscores = backward_scores(attn_probs, d_att, row_delta, value_sets)
    query_grad = grad_queries(dscores, key_sets)
    key_contrib = contract_keys(dscores, query_tiles)
    value_contrib = contract_keys(probs_low, d_att)
    key_pad = from_blocks(
        add_into(key_contrib, own_place, own_usable, pad_count), pad_rows, pad_cols
    )
    value_pad = from_blocks(
        add_into(value_contrib, own_place, own_usable, pad_count), pad_rows, pad_cols
    )
    pad_terms = jnp.stack((key_pad, value_pad))
    extended = padded_2(pad_terms.astype(jnp.bfloat16), (("lat", 1), ("lon", 2)), BLK).astype(
        pad_terms.dtype
    )
    folded = fold_joint(extended, lat_rows, lon_cols)
    key_grad = folded[0].astype(jnp.bfloat16)
    value_grad = folded[1].astype(jnp.bfloat16)
    mixed_out = from_blocks(mixed_flat.reshape(attended.shape), lat_blocks, lon_blocks)
    q_grad = from_blocks(query_grad, lat_blocks, lon_blocks)
    return (mixed_out, q_grad, key_grad, value_grad, w_grad)


def solution(mesh):
    return jax.shard_map(
        on_device,
        mesh=mesh,
        in_specs=(
            P("lat", "lon", None),
            P("lat", "lon", None),
            P("lat", "lon", None),
            P("lat", "lon", None),
            P(),
            P(),
            P(),
        ),
        out_specs=(
            P("lat", "lon", None),
            P("lat", "lon", None),
            P("lat", "lon", None),
            P("lat", "lon", None),
            P(),
        ),
        check_vma=False,
    )
```

profile of v0, /device:TPU:0, one launch (start us, length us, event | category | flops | bytes accessed | tf_op | source)
XLA Modules:
  0.0 270.1 jit_solution(14660080153096011954)
XLA Ops:
  7.2 1.2 fusion.18
  8.4 4.0 %collective-permute-start.1 = (bf16[2,8,8,768]{3,2,1,0:T(8,128)(2,1)S(1)}, bf16[2,8,8,768]{3,2,1,0:T(8,128)(2,1)S(1)}, u32[]{:S(2)}, u32[]{:S(2)}) collective-permute-start(bf16[2,8,8,768]{3,2,1,0:T(8,128)(2,1)S(1)} %get-tuple-element.152), channel_id=1, source_target_pairs={{8,0},{16,8},{24,16},{0,24},{9,1},{17,9},{25,17},{1,25},{10,2},{18... | collective-permute-start | bytes 589832 | tf_op jit(solution)/shard_map/ppermute | solution.py:21
  12.5 1.3 gather_fusion.1
  13.8 1.2 gather_fusion
  15.5 1.5 convolution_convert_fusion.2
  17.7 4.1 %collective-permute-done = bf16[2,8,8,768]{3,2,1,0:T(8,128)(2,1)S(1)} collective-permute-done((bf16[2,8,8,768]{3,2,1,0:T(8,128)(2,1)S(1)}, bf16[2,8,8,768]{3,2,1,0:T(8,128)(2,1)S(1)}, u32[]{:S(2)}, u32[]{:S(2)}) %collective-permute-start) | collective-permute-done | bytes 196640 | tf_op jit(solution)/shard_map/ppermute | solution.py:20
  22.8 2.2 collective-permute-start.3
  25.7 1.1 copy.42
  26.8 1.3 reshape_reshape_transpose_reshape.7
  28.1 1.1 copy.45
  30.0 12.1 %collective-permute-done.3 = bf16[2,32,8,768]{3,2,1,0:T(8,128)(2,1)S(1)} collective-permute-done((bf16[2,32,8,768]{3,2,1,0:T(8,128)(2,1)}, bf16[2,32,8,768]{3,2,1,0:T(8,128)(2,1)S(1)}, u32[]{:S(2)}, u32[]{:S(2)}) %collective-permute-start.3) | collective-permute-done | bytes 786464 | tf_op jit(solution)/shard_map/ppermute | solution.py:21
  42.1 3.0 %collective-permute-done.2 = bf16[2,32,8,768]{3,2,1,0:T(8,128)(2,1)} collective-permute-done((bf16[2,32,8,768]{3,2,1,0:T(8,128)(2,1)}, bf16[2,32,8,768]{3,2,1,0:T(8,128)(2,1)}, u32[]{:S(2)}, u32[]{:S(2)}) %collective-permute-start.2) | collective-permute-done | bytes 786464 | tf_op jit(solution)/shard_map/ppermute | solution.py:20
  45.1 1.3 pad_maximum_fusion
  46.7 1.5 gather_fusion.3
  48.2 1.5 gather_fusion.2
  49.7 2.5 broadcast_select_fusion.2
  52.2 2.7 %reshape.774 = bf16[2,256,12,64]{3,2,1,0:T(8,128)(2,1)S(1)} reshape(bf16[8,64,768]{2,1,0:T(8,128)(2,1)} %get-tuple-element.156) | data formatting | bytes 1572864 | tf_op jit(solution)/shard_map/reshape;reshape | solution.py:43
  54.9 2.1 copy.37
  57.1 2.7 %reshape.775 = bf16[2,256,12,64]{3,2,1,0:T(8,128)(2,1)S(1)} reshape(bf16[8,64,768]{2,1,0:T(8,128)(2,1)} %get-tuple-element.155) | data formatting | bytes 1572864 | tf_op jit(solution)/shard_map/reshape;reshape | solution.py:43
  59.8 2.1 copy.35
  62.0 1.8 bitcast_reduce_fusion
  65.5 1.3 multiply_reduce_fusion
  68.4 1.5 convolution_bitcast_fusion
  69.9 4.7 %copy.46 = f32[2,256,12,64]{3,2,1,0:T(8,128)} copy(f32[2,256,12,64]{1,3,2,0:T(8,128)} %convolution_bitcast_fusion) | data formatting | bytes 3145728 | tf_op jit(solution)/shard_map/nhqk,nqhd->nkhd/transpose | solution.py:133
  74.6 4.4 %reshape_reshape.37 = f32[8,49152]{1,0:T(8,128)} reshape(f32[2,256,12,64]{3,2,1,0:T(8,128)} %copy.46) | data formatting | bytes 3145728 | tf_op jit(solution)/shard_map/reshape;reshape | solution.py:142
  79.0 3.7 %copy.49 = f32[2,256,12,64]{3,2,1,0:T(8,128)} copy(f32[2,256,12,64]{1,3,2,0:T(8,128)S(1)} %convolution_bitcast_fusion.1) | data formatting | bytes 3145728 | tf_op jit(solution)/shard_map/nhqk,nqhd->nkhd/transpose | solution.py:133
  82.8 4.5 %reshape_reshape.39 = f32[8,49152]{1,0:T(8,128)} reshape(f32[2,256,12,64]{3,2,1,0:T(8,128)} %copy.49) | data formatting | bytes 3145728 | tf_op jit(solution)/shard_map/reshape;reshape | solution.py:142
  87.3 3.4 %broadcast_select_fusion.1 = (f32[8,49152]{1,0:T(8,128)}, f32[8,49152]{1,0:T(8,128)}) fusion(f32[8,49152]{1,0:T(8,128)S(1)} %copy-done.6, pred[8]{0:T(512)(128)(4,1)S(1)} %get-tuple-element.142, f32[8,49152]{1,0:T(8,128)} %reshape_reshape.39), kind=kLoop, calls=%fused_computation.38 | loop fusion | flops 786432 | bytes 6291464 | tf_op jit(solution)/shard_map/jit(_where)/select_n | solution.py:143
  90.7 5.1 %scatter_custom_fusion.1 = f32[12,49152]{1,0:T(8,128)} fusion(s32[8]{0:T(128)} %fusion.33, f32[8,49152]{1,0:T(8,128)} %get-tuple-element.154, f32[]{:T(128)} %constant.347.clone.1), kind=kCustom, calls=%fused_computation.13 | custom fusion | flops 393216 | bytes 2359808 | tf_op jit(solution)/shard_map/scatter-add | solution.py:145
  95.7 2.0 convert.17
  98.3 4.9 %scatter_custom_fusion = f32[12,49152]{1,0:T(8,128)} fusion(s32[8]{0:T(128)} %fusion.33, f32[8,49152]{1,0:T(8,128)} %get-tuple-element.153, f32[]{:T(128)} %constant.347.clone.1), kind=kCustom, calls=%fused_computation.15 | custom fusion | flops 393216 | bytes 2359808 | tf_op jit(solution)/shard_map/scatter-add | solution.py:145
  103.2 2.0 convert.16
  105.8 1.1 pad_maximum_fusion.7
  106.9 1.4 collective-permute-start.5
  108.9 1.2 copy.38
  110.1 1.9 reshape_reshape.35
  112.0 2.9 %fusion.19 = f32[768,768]{1,0:T(8,128)} fusion(bf16[128,768]{0,1:T(8,128)(2,1)} %reshape_reshape.35, bf16[16,8,768]{2,1,0:T(8,128)(2,1)} %param.32), kind=kOutput, calls=%fused_computation.71 | convolution fusion | flops 150994944 | bytes 2752512 | tf_op jit(solution)/shard_map/dot_general | solution.py:206
  114.9 10.2 %collective-permute-done.5 = bf16[2,8,24,768]{3,2,1,0:T(8,128)(2,1)} collective-permute-done((bf16[2,8,24,768]{3,2,1,0:T(8,128)(2,1)}, bf16[2,8,24,768]{3,2,1,0:T(8,128)(2,1)}, u32[]{:S(2)}, u32[]{:S(2)}) %collective-permute-start.5) | collective-permute-done | bytes 589856 | tf_op jit(solution)/shard_map/ppermute | solution.py:21
  125.1 10.0 %collective-permute-done.4 = bf16[2,8,24,768]{3,2,1,0:T(8,128)(2,1)} collective-permute-done((bf16[2,8,24,768]{3,2,1,0:T(8,128)(2,1)}, bf16[2,8,24,768]{3,2,1,0:T(8,128)(2,1)}, u32[]{:S(2)}, u32[]{:S(2)}) %collective-permute-start.4) | collective-permute-done | bytes 589856 | tf_op jit(solution)/shard_map/ppermute | solution.py:20
  135.1 2.8 %pad_maximum_fusion.4 = (bf16[2,48,8,768]{3,2,1,0:T(8,128)(2,1)}, bf16[2,48,8,768]{3,2,1,0:T(8,128)(2,1)}) fusion(bf16[2,8,24,768]{3,2,1,0:T(8,128)(2,1)} %collective-permute-done.5, bf16[2,8,24,768]{3,2,1,0:T(8,128)(2,1)} %collective-permute-done.4, bf16[1,32,24,768]{3,2,1,0:T(8,128)(2,1)S(1)} %bitcast.90, bf16[1,32,24,768]{3,2,1,0:T(8,128)(2,1)S(1)} %bitcast.100), kind=kLoop, calls=%fused_computation.29 | loop fusion | flops 9437184 | bytes 5898240 | tf_op jit(solution)/shard_map/slice | solution.py:18
  137.9 4.1 %collective-permute-start.7 = (bf16[2,48,8,768]{3,2,1,0:T(8,128)(2,1)}, bf16[2,48,8,768]{3,2,1,0:T(8,128)(2,1)}, u32[]{:S(2)}, u32[]{:S(2)}) collective-permute-start(bf16[2,48,8,768]{3,2,1,0:T(8,128)(2,1)} %get-tuple-element.144), channel_id=1, source_target_pairs={{1,0},{2,1},{3,2},{4,3},{5,4},{6,5},{7,6},{0,7},{9,8},{10,9},{11,1... | collective-permute-start | bytes 3538952 | tf_op jit(solution)/shard_map/ppermute | solution.py:21
  142.0 1.1 fusion.9
  143.1 2.2 copy.44
  145.3 2.1 reshape_transpose_reshape_reshape.7
  147.4 2.0 fusion.10
  149.3 102.2 %all-reduce.2.cloned.1.call-done = f32[768,768]{1,0:T(8,128)} async-done(((f32[768,768]{1,0:T(8,128)}), f32[768,768]{1,0:T(8,128)}) %all-reduce.2.cloned.1.call-update) | async-done | bytes 2359312 | tf_op jit(solution)/shard_map/psum | solution.py:209
  251.6 3.2 %broadcast_multiply_fusion = f32[768,768]{1,0:T(8,128)} fusion(f32[768,768]{1,0:T(8,128)} %all-reduce.2.cloned.1.call-done), kind=kLoop, calls=%fused_computation.30 | loop fusion | flops 589824 | bytes 4718592 | tf_op jit(solution)/shard_map/div | solution.py:209
  256.9 1.3 convert_add_fusion
  (77 shorter events, 16.2 us)
Async XLA Ops:
  7.2 8.3 %copy-start = (bf16[768,768]{1,0:T(8,128)(2,1)S(1)}, bf16[768,768]{1,0:T(8,128)(2,1)}, u32[]{:S(2)}) copy-start(bf16[768,768]{1,0:T(8,128)(2,1)} %param.33) | copy-start | bytes 3538948
  7.2 14.6 %copy-start.9 = (bf16[16,8,768]{2,1,0:T(8,128)(2,1)S(1)}, bf16[16,8,768]{2,1,0:T(8,128)(2,1)}, u32[]{:S(2)}) copy-start(bf16[16,8,768]{2,1,0:T(8,128)(2,1)} %param.30) | copy-start | bytes 589828
  7.2 14.6 %copy-start.10 = (bf16[16,8,768]{2,1,0:T(8,128)(2,1)S(1)}, bf16[16,8,768]{2,1,0:T(8,128)(2,1)}, u32[]{:S(2)}) copy-start(bf16[16,8,768]{2,1,0:T(8,128)(2,1)} %param.31) | copy-start | bytes 589828
  7.2 244.4 %all-reduce.2.cloned.1.call-start = ((), (), s32[]{:S(2)}) async-start(), calls=%async_computation | async-start | bytes 4718592 | tf_op jit(solution)/shard_map/psum | solution.py:209
  8.4 9.3 %collective-permute-start.1 = (bf16[2,8,8,768]{3,2,1,0:T(8,128)(2,1)S(1)}, bf16[2,8,8,768]{3,2,1,0:T(8,128)(2,1)S(1)}, u32[]{:S(2)}, u32[]{:S(2)}) collective-permute-start(bf16[2,8,8,768]{3,2,1,0:T(8,128)(2,1)S(1)} %get-tuple-element.152), channel_id=1, source_target_pairs={{8,0},{16,8},{24,16},{0,24},{9,1},{17,9},{25,17},{1,25},{10,2},{18... | collective-permute-start | bytes 589832 | tf_op jit(solution)/shard_map/ppermute | solution.py:21
  12.4 9.4 %collective-permute-start = (bf16[2,8,8,768]{3,2,1,0:T(8,128)(2,1)S(1)}, bf16[2,8,8,768]{3,2,1,0:T(8,128)(2,1)S(1)}, u32[]{:S(2)}, u32[]{:S(2)}) collective-permute-start(bf16[2,8,8,768]{3,2,1,0:T(8,128)(2,1)S(1)} %get-tuple-element.151), channel_id=1, source_target_pairs={{0,8},{8,16},{16,24},{24,0},{1,9},{9,17},{17,25},{25,1},{2,10},{10... | collective-permute-start | bytes 589832 | tf_op jit(solution)/shard_map/ppermute | solution.py:20
  22.8 19.3 %collective-permute-start.3 = (bf16[2,32,8,768]{3,2,1,0:T(8,128)(2,1)}, bf16[2,32,8,768]{3,2,1,0:T(8,128)(2,1)S(1)}, u32[]{:S(2)}, u32[]{:S(2)}) collective-permute-start(bf16[2,32,8,768]{3,2,1,0:T(8,128)(2,1)} %pad_maximum_fusion.5), channel_id=1, source_target_pairs={{1,0},{2,1},{3,2},{4,3},{5,4},{6,5},{7,6},{0,7},{9,8},{10,9},{11,1... | collective-permute-start | bytes 2359304 | tf_op jit(solution)/shard_map/ppermute | solution.py:21
  24.9 20.1 %collective-permute-start.2 = (bf16[2,32,8,768]{3,2,1,0:T(8,128)(2,1)}, bf16[2,32,8,768]{3,2,1,0:T(8,128)(2,1)}, u32[]{:S(2)}, u32[]{:S(2)}) collective-permute-start(bf16[2,32,8,768]{3,2,1,0:T(8,128)(2,1)} %pad_maximum_fusion.5), channel_id=1, source_target_pairs={{0,1},{1,2},{2,3},{3,4},{4,5},{5,6},{6,7},{7,0},{8,9},{9,10},{10,1... | collective-permute-start | bytes 2359304 | tf_op jit(solution)/shard_map/ppermute | solution.py:20
  48.2 1.5 copy-start.8
  62.0 2.4 copy-start.5
  64.3 1.1 copy-start.3
  66.7 1.7 copy-start.7
  67.4 1.0 copy-start.1
  82.8 4.5 %copy-start.6 = (f32[8,49152]{1,0:T(8,128)S(1)}, f32[8,49152]{1,0:T(8,128)}, u32[]{:S(2)}) copy-start(f32[8,49152]{1,0:T(8,128)} %reshape_reshape.37) | copy-start | bytes 4718596
  105.7 3.2 %copy-start.11 = (bf16[2,64,12,64]{1,3,2,0:T(8,128)(2,1)S(1)}, bf16[2,64,12,64]{1,3,2,0:T(8,128)(2,1)}, u32[]{:S(2)}) copy-start(bf16[2,64,12,64]{1,3,2,0:T(8,128)(2,1)} %get-tuple-element.162) | copy-start | bytes 589828
  106.9 18.2 %collective-permute-start.5 = (bf16[2,8,24,768]{3,2,1,0:T(8,128)(2,1)}, bf16[2,8,24,768]{3,2,1,0:T(8,128)(2,1)}, u32[]{:S(2)}, u32[]{:S(2)}) collective-permute-start(bf16[2,8,24,768]{3,2,1,0:T(8,128)(2,1)} %get-tuple-element.146), channel_id=1, source_target_pairs={{8,0},{16,8},{24,16},{0,24},{9,1},{17,9},{25,17},{1,25},{10,2},{18... | collective-permute-start | bytes 1769480 | tf_op jit(solution)/shard_map/ppermute | solution.py:21
  108.3 26.7 %collective-permute-start.4 = (bf16[2,8,24,768]{3,2,1,0:T(8,128)(2,1)}, bf16[2,8,24,768]{3,2,1,0:T(8,128)(2,1)}, u32[]{:S(2)}, u32[]{:S(2)}) collective-permute-start(bf16[2,8,24,768]{3,2,1,0:T(8,128)(2,1)} %get-tuple-element.145), channel_id=1, source_target_pairs={{0,8},{8,16},{16,24},{24,0},{1,9},{9,17},{17,25},{25,1},{2,10},{10... | collective-permute-start | bytes 1769480 | tf_op jit(solution)/shard_map/ppermute | solution.py:20
  114.9 27.1 %copy-start.2 = (bf16[2,12,64,256]{3,2,1,0:T(8,128)(2,1)S(1)}, bf16[2,12,64,256]{3,2,1,0:T(8,128)(2,1)}, u32[]{:S(2)}) copy-start(bf16[2,12,64,256]{3,2,1,0:T(8,128)(2,1)} %copy-done.1) | copy-start | bytes 2359300
  114.9 27.1 %copy-start.4 = (bf16[2,256,12,64]{1,3,2,0:T(8,128)(2,1)S(1)}, bf16[2,256,12,64]{1,3,2,0:T(8,128)(2,1)}, u32[]{:S(2)}) copy-start(bf16[2,256,12,64]{1,3,2,0:T(8,128)(2,1)} %copy.35) | copy-start | bytes 2359300
  137.9 116.9 %collective-permute-start.7 = (bf16[2,48,8,768]{3,2,1,0:T(8,128)(2,1)}, bf16[2,48,8,768]{3,2,1,0:T(8,128)(2,1)}, u32[]{:S(2)}, u32[]{:S(2)}) collective-permute-start(bf16[2,48,8,768]{3,2,1,0:T(8,128)(2,1)} %get-tuple-element.144), channel_id=1, source_target_pairs={{1,0},{2,1},{3,2},{4,3},{5,4},{6,5},{7,6},{0,7},{9,8},{10,9},{11,1... | collective-permute-start | bytes 3538952 | tf_op jit(solution)/shard_map/ppermute | solution.py:21
  142.0 112.8 %collective-permute-start.6 = (bf16[2,48,8,768]{3,2,1,0:T(8,128)(2,1)}, bf16[2,48,8,768]{3,2,1,0:T(8,128)(2,1)}, u32[]{:S(2)}, u32[]{:S(2)}) collective-permute-start(bf16[2,48,8,768]{3,2,1,0:T(8,128)(2,1)} %get-tuple-element.143), channel_id=1, source_target_pairs={{0,1},{1,2},{2,3},{3,4},{4,5},{5,6},{6,7},{7,0},{8,9},{9,10},{10,1... | collective-permute-start | bytes 3538952 | tf_op jit(solution)/shard_map/ppermute | solution.py:20
Sparse Core Ops, SparseCore 0:
  115.0 136.5 all-reduce.1
where the time goes:
time: 271 us; the launch traced here: 270 us
  waiting for transfers between devices  142 us (52%)
  local copies, waits for them, and re-layouts  48.2 us (18%)
  other arithmetic  39.8 us (15%)
  between operations  14.4 us (5%)
  matrix products  13.1 us (5%)
  starting transfers between devices  12.4 us (5%)
    psum x1, waiting for transfers between devices, on_device(): w_grad = lax.psum(local_weight, ('lat', 'lon')) / math.sqrt(tokens_all)  102 us
    ppermute x4, waiting for transfers between devices, padded_2(): after = lax.ppermute(leading, axis, down)  23 us
    ppermute x4, waiting for transfers between devices, padded_2(): before = lax.ppermute(last, axis, up)  17.1 us
    another operation x8, local copies, waits for them, and re-layouts, split_heads(): block_tiles.reshape(block_tiles.shape[0], block_tiles.shape[1], HEADS, HE...  13.6 us
    ppermute x4, starting transfers between devices, padded_2(): after = lax.ppermute(leading, axis, down)  11.7 us
    scatter-add x2, other arithmetic, add_into(): jnp.zeros((pad_count, BLK * BLK * feat_width), jnp.float32).at[flat_place]  9.96 us
    another operation x2, local copies, waits for them, and re-layouts, add_into(): flat_terms = contrib.reshape(flat_place.shape[0], BLK * BLK * feat_width)  8.94 us
    transpose x2, local copies, waits for them, and re-layouts, contract_keys(): jnp.einsum('nhqk,nqhd->nkhd', weights_low, split_heads(block_tiles), pref...  8.46 us
  transfers between devices with their start and end apart: 9, of which 7 were waited for; matrix products, arithmetic and copies ran while one was open for 11% of the time, Pallas kernels for 0%

commit v1 on v0

--- a/solution.py
+++ b/solution.py
@@ -206,7 +206,7 @@
     local_weight = lax.dot_general(
         flat_att, flat_grad, (((0,), (0,)), ((), ())), preferred_element_type=jnp.float32
     )
-    w_grad = lax.psum(local_weight, ("lat", "lon")) / math.sqrt(tokens_all)
+    w_grad = lax.psum(lax.psum(local_weight, "lon"), "lat") / math.sqrt(tokens_all)
     d_att = lax.dot_general(
         flat_grad, w_out, (((1,), (1,)), ((), ())), preferred_element_type=jnp.float32
     )

time: 271 us -> 281 us (1.037)
  waiting for transfers between devices: 142 us -> 151 us
    psum x1 -> x2, waiting for transfers between devices: 102 us -> 115 us  [the longest x1 58.7 us: on_device(): lax.psum(lax.psum(local_weight, 'lon'), 'lat') / math.sqrt(tokens_all)]
  transfers between devices with their start and end apart: 9 -> 10, of which waited for: 7 -> 8; matrix products, arithmetic and copies ran while one was open for 11% -> 13% of each run, Pallas kernels for 0% -> 0%
where the time goes in v1:
time: 281 us; the launch traced here: 280 us
  waiting for transfers between devices  151 us (54%)
  local copies, waits for them, and re-layouts  48.1 us (17%)
  other arithmetic  39.9 us (14%)
  matrix products  14.6 us (5%)
  between operations  14.4 us (5%)
  starting transfers between devices  11.8 us (4%)
    psum x1, waiting for transfers between devices, on_device(): lax.psum(lax.psum(local_weight, 'lon'), 'lat') / math.sqrt(tokens_all)  58.7 us
    psum x1, waiting for transfers between devices, on_device(): lax.psum(local_weight, 'lon')  56.5 us
    ppermute x4, waiting for transfers between devices, padded_2(): after = lax.ppermute(leading, axis, down)  21.2 us
    ppermute x4, waiting for transfers between devices, padded_2(): before = lax.ppermute(last, axis, up)  14.6 us
    another operation x8, local copies, waits for them, and re-layouts, split_heads(): block_tiles.reshape(block_tiles.shape[0], block_tiles.shape[1], HEADS, HE...  13.6 us
    ppermute x4, starting transfers between devices, padded_2(): after = lax.ppermute(leading, axis, down)  11.1 us
    scatter-add x2, other arithmetic, add_into(): jnp.zeros((pad_count, BLK * BLK * feat_width), jnp.float32).at[flat_place]  9.98 us
    another operation x2, local copies, waits for them, and re-layouts, add_into(): flat_terms = contrib.reshape(flat_place.shape[0], BLK * BLK * feat_width)  8.94 us
  transfers between devices with their start and end apart: 10, of which 8 were waited for; matrix products, arithmetic and copies ran while one was open for 13% of the time, Pallas kernels for 0%

profile of v1, /device:TPU:0, one launch (start us, length us, event | category | flops | bytes accessed | tf_op | source)
XLA Modules:
  0.0 279.8 jit_solution(17389488359421213702)
XLA Ops:
  7.2 1.2 fusion.18
  8.4 4.0 %collective-permute-start.1 = (bf16[2,8,8,768]{3,2,1,0:T(8,128)(2,1)S(1)}, bf16[2,8,8,768]{3,2,1,0:T(8,128)(2,1)S(1)}, u32[]{:S(2)}, u32[]{:S(2)}) collective-permute-start(bf16[2,8,8,768]{3,2,1,0:T(8,128)(2,1)S(1)} %get-tuple-element.152), channel_id=1, source_target_pairs={{8,0},{16,8},{24,16},{0,24},{9,1},{17,9},{25,17},{1,25},{10,2},{18... | collective-permute-start | bytes 589832 | tf_op jit(solution)/shard_map/ppermute | solution.py:21
  12.5 1.3 gather_fusion.1
  13.8 1.2 gather_fusion
  15.5 1.5 convolution_convert_fusion.2
  17.7 4.1 %collective-permute-done = bf16[2,8,8,768]{3,2,1,0:T(8,128)(2,1)S(1)} collective-permute-done((bf16[2,8,8,768]{3,2,1,0:T(8,128)(2,1)S(1)}, bf16[2,8,8,768]{3,2,1,0:T(8,128)(2,1)S(1)}, u32[]{:S(2)}, u32[]{:S(2)}) %collective-permute-start) | collective-permute-done | bytes 196640 | tf_op jit(solution)/shard_map/ppermute | solution.py:20
  22.8 2.2 collective-permute-start.3
  25.7 1.1 copy.42
  26.8 1.3 reshape_reshape_transpose_reshape.7
  28.1 1.1 copy.45
  30.0 12.1 %collective-permute-done.3 = bf16[2,32,8,768]{3,2,1,0:T(8,128)(2,1)S(1)} collective-permute-done((bf16[2,32,8,768]{3,2,1,0:T(8,128)(2,1)}, bf16[2,32,8,768]{3,2,1,0:T(8,128)(2,1)S(1)}, u32[]{:S(2)}, u32[]{:S(2)}) %collective-permute-start.3) | collective-permute-done | bytes 786464 | tf_op jit(solution)/shard_map/ppermute | solution.py:21
  42.1 3.0 %collective-permute-done.2 = bf16[2,32,8,768]{3,2,1,0:T(8,128)(2,1)} collective-permute-done((bf16[2,32,8,768]{3,2,1,0:T(8,128)(2,1)}, bf16[2,32,8,768]{3,2,1,0:T(8,128)(2,1)}, u32[]{:S(2)}, u32[]{:S(2)}) %collective-permute-start.2) | collective-permute-done | bytes 786464 | tf_op jit(solution)/shard_map/ppermute | solution.py:20
  45.1 1.3 pad_maximum_fusion
  46.7 1.5 gather_fusion.3
  48.2 1.5 gather_fusion.2
  49.7 2.5 broadcast_select_fusion.2
  52.2 2.7 reshape.774
  54.9 2.1 copy.37
  57.1 2.7 reshape.775
  59.8 2.1 copy.35
  61.9 1.8 bitcast_reduce_fusion
  65.4 1.3 multiply_reduce_fusion
  68.3 1.5 convolution_bitcast_fusion
  69.8 4.7 %copy.46 = f32[2,256,12,64]{3,2,1,0:T(8,128)} copy(f32[2,256,12,64]{1,3,2,0:T(8,128)} %convolution_bitcast_fusion) | data formatting | bytes 3145728 | tf_op jit(solution)/shard_map/nhqk,nqhd->nkhd/transpose | solution.py:133
  74.5 4.4 %reshape_reshape.37 = f32[8,49152]{1,0:T(8,128)} reshape(f32[2,256,12,64]{3,2,1,0:T(8,128)} %copy.46) | data formatting | bytes 3145728 | tf_op jit(solution)/shard_map/reshape;reshape | solution.py:142
  78.9 3.7 %copy.49 = f32[2,256,12,64]{3,2,1,0:T(8,128)} copy(f32[2,256,12,64]{1,3,2,0:T(8,128)S(1)} %convolution_bitcast_fusion.1) | data formatting | bytes 3145728 | tf_op jit(solution)/shard_map/nhqk,nqhd->nkhd/transpose | solution.py:133
  82.7 4.6 %reshape_reshape.39 = f32[8,49152]{1,0:T(8,128)} reshape(f32[2,256,12,64]{3,2,1,0:T(8,128)} %copy.49) | data formatting | bytes 3145728 | tf_op jit(solution)/shard_map/reshape;reshape | solution.py:142
  87.2 3.4 %broadcast_select_fusion.1 = (f32[8,49152]{1,0:T(8,128)}, f32[8,49152]{1,0:T(8,128)}) fusion(f32[8,49152]{1,0:T(8,128)S(1)} %copy-done.4, pred[8]{0:T(512)(128)(4,1)S(1)} %get-tuple-element.142, f32[8,49152]{1,0:T(8,128)} %reshape_reshape.39), kind=kLoop, calls=%fused_computation.38 | loop fusion | flops 786432 | bytes 6291464 | tf_op jit(solution)/shard_map/jit(_where)/select_n | solution.py:143
  90.6 5.1 %scatter_custom_fusion.1 = f32[12,49152]{1,0:T(8,128)} fusion(s32[8]{0:T(128)} %fusion.33, f32[8,49152]{1,0:T(8,128)} %get-tuple-element.154, f32[]{:T(128)} %constant.347.clone.1), kind=kCustom, calls=%fused_computation.13 | custom fusion | flops 393216 | bytes 2359808 | tf_op jit(solution)/shard_map/scatter-add | solution.py:145
  95.7 2.0 convert.17
  98.2 4.9 %scatter_custom_fusion = f32[12,49152]{1,0:T(8,128)} fusion(s32[8]{0:T(128)} %fusion.33, f32[8,49152]{1,0:T(8,128)} %get-tuple-element.153, f32[]{:T(128)} %constant.347.clone.1), kind=kCustom, calls=%fused_computation.15 | custom fusion | flops 393216 | bytes 2359808 | tf_op jit(solution)/shard_map/scatter-add | solution.py:145
  103.1 2.0 convert.16
  106.8 1.4 collective-permute-start.5
  108.9 1.2 copy.38
  110.0 1.9 reshape_reshape.35
  111.9 2.9 %fusion.19 = f32[768,768]{1,0:T(8,128)} fusion(bf16[128,768]{0,1:T(8,128)(2,1)} %reshape_reshape.35, bf16[16,8,768]{2,1,0:T(8,128)(2,1)} %param.32), kind=kOutput, calls=%fused_computation.71 | convolution fusion | flops 150994944 | bytes 2752512 | tf_op jit(solution)/shard_map/dot_general | solution.py:206
  114.9 8.5 %collective-permute-done.5 = bf16[2,8,24,768]{3,2,1,0:T(8,128)(2,1)} collective-permute-done((bf16[2,8,24,768]{3,2,1,0:T(8,128)(2,1)}, bf16[2,8,24,768]{3,2,1,0:T(8,128)(2,1)}, u32[]{:S(2)}, u32[]{:S(2)}) %collective-permute-start.5) | collective-permute-done | bytes 589856 | tf_op jit(solution)/shard_map/ppermute | solution.py:21
  123.4 7.5 %collective-permute-done.4 = bf16[2,8,24,768]{3,2,1,0:T(8,128)(2,1)} collective-permute-done((bf16[2,8,24,768]{3,2,1,0:T(8,128)(2,1)}, bf16[2,8,24,768]{3,2,1,0:T(8,128)(2,1)}, u32[]{:S(2)}, u32[]{:S(2)}) %collective-permute-start.4) | collective-permute-done | bytes 589856 | tf_op jit(solution)/shard_map/ppermute | solution.py:20
  130.8 2.9 %pad_maximum_fusion.4 = (bf16[2,48,8,768]{3,2,1,0:T(8,128)(2,1)}, bf16[2,48,8,768]{3,2,1,0:T(8,128)(2,1)}) fusion(bf16[2,8,24,768]{3,2,1,0:T(8,128)(2,1)} %collective-permute-done.5, bf16[2,8,24,768]{3,2,1,0:T(8,128)(2,1)} %collective-permute-done.4, bf16[1,32,24,768]{3,2,1,0:T(8,128)(2,1)S(1)} %bitcast.90, bf16[1,32,24,768]{3,2,1,0:T(8,128)(2,1)S(1)} %bitcast.100), kind=kLoop, calls=%fused_computation.29 | loop fusion | flops 9437184 | bytes 5898240 | tf_op jit(solution)/shard_map/slice | solution.py:18
  133.7 3.5 %collective-permute-start.7 = (bf16[2,48,8,768]{3,2,1,0:T(8,128)(2,1)}, bf16[2,48,8,768]{3,2,1,0:T(8,128)(2,1)}, u32[]{:S(2)}, u32[]{:S(2)}) collective-permute-start(bf16[2,48,8,768]{3,2,1,0:T(8,128)(2,1)} %get-tuple-element.144), channel_id=1, source_target_pairs={{1,0},{2,1},{3,2},{4,3},{5,4},{6,5},{7,6},{0,7},{9,8},{10,9},{11,1... | collective-permute-start | bytes 3538952 | tf_op jit(solution)/shard_map/ppermute | solution.py:21
  137.2 56.5 %all-reduce.3.cloned.1.call-done = f32[768,768]{1,0:T(8,128)} async-done(((f32[768,768]{1,0:T(8,128)}), f32[768,768]{1,0:T(8,128)}) %all-reduce.3.cloned.1.call-update) | async-done | bytes 2359312 | tf_op jit(solution)/shard_map/psum | solution.py:209
  193.8 2.5 fusion.9
  196.3 2.2 copy.44
  198.5 2.1 reshape_transpose_reshape_reshape.7
  200.5 2.0 fusion.10
  204.6 1.3 convert_add_fusion
  211.1 58.7 %all-reduce.5.cloned.1.call-done = f32[768,768]{1,0:T(8,128)} async-done(((f32[768,768]{1,0:T(8,128)}), f32[768,768]{1,0:T(8,128)}) %all-reduce.5.cloned.1.call-update) | async-done | bytes 2359312 | tf_op jit(solution)/shard_map/psum | solution.py:209
  269.8 3.2 %broadcast_multiply_fusion = f32[768,768]{1,0:T(8,128)} fusion(f32[768,768]{1,0:T(8,128)} %all-reduce.5.cloned.1.call-done), kind=kLoop, calls=%fused_computation.30 | loop fusion | flops 589824 | bytes 4718592 | tf_op jit(solution)/shard_map/div | solution.py:209
  (76 shorter events, 17.3 us)
Async XLA Ops:
  7.2 8.3 %copy-start = (bf16[768,768]{1,0:T(8,128)(2,1)S(1)}, bf16[768,768]{1,0:T(8,128)(2,1)}, u32[]{:S(2)}) copy-start(bf16[768,768]{1,0:T(8,128)(2,1)} %param.33) | copy-start | bytes 3538948
  7.2 14.6 %copy-start.7 = (bf16[16,8,768]{2,1,0:T(8,128)(2,1)S(1)}, bf16[16,8,768]{2,1,0:T(8,128)(2,1)}, u32[]{:S(2)}) copy-start(bf16[16,8,768]{2,1,0:T(8,128)(2,1)} %param.30) | copy-start | bytes 589828
  7.2 14.6 %copy-start.8 = (bf16[16,8,768]{2,1,0:T(8,128)(2,1)S(1)}, bf16[16,8,768]{2,1,0:T(8,128)(2,1)}, u32[]{:S(2)}) copy-start(bf16[16,8,768]{2,1,0:T(8,128)(2,1)} %param.31) | copy-start | bytes 589828
  7.2 186.6 %all-reduce.3.cloned.1.call-start = ((), (), s32[]{:S(2)}) async-start(), calls=%async_computation | async-start | bytes 4718592 | tf_op jit(solution)/shard_map/psum | solution.py:209
  8.4 9.3 %collective-permute-start.1 = (bf16[2,8,8,768]{3,2,1,0:T(8,128)(2,1)S(1)}, bf16[2,8,8,768]{3,2,1,0:T(8,128)(2,1)S(1)}, u32[]{:S(2)}, u32[]{:S(2)}) collective-permute-start(bf16[2,8,8,768]{3,2,1,0:T(8,128)(2,1)S(1)} %get-tuple-element.152), channel_id=1, source_target_pairs={{8,0},{16,8},{24,16},{0,24},{9,1},{17,9},{25,17},{1,25},{10,2},{18... | collective-permute-start | bytes 589832 | tf_op jit(solution)/shard_map/ppermute | solution.py:21
  12.4 9.4 %collective-permute-start = (bf16[2,8,8,768]{3,2,1,0:T(8,128)(2,1)S(1)}, bf16[2,8,8,768]{3,2,1,0:T(8,128)(2,1)S(1)}, u32[]{:S(2)}, u32[]{:S(2)}) collective-permute-start(bf16[2,8,8,768]{3,2,1,0:T(8,128)(2,1)S(1)} %get-tuple-element.151), channel_id=1, source_target_pairs={{0,8},{8,16},{16,24},{24,0},{1,9},{9,17},{17,25},{25,1},{2,10},{10... | collective-permute-start | bytes 589832 | tf_op jit(solution)/shard_map/ppermute | solution.py:20
  22.8 19.3 %collective-permute-start.3 = (bf16[2,32,8,768]{3,2,1,0:T(8,128)(2,1)}, bf16[2,32,8,768]{3,2,1,0:T(8,128)(2,1)S(1)}, u32[]{:S(2)}, u32[]{:S(2)}) collective-permute-start(bf16[2,32,8,768]{3,2,1,0:T(8,128)(2,1)} %pad_maximum_fusion.5), channel_id=1, source_target_pairs={{1,0},{2,1},{3,2},{4,3},{5,4},{6,5},{7,6},{0,7},{9,8},{10,9},{11,1... | collective-permute-start | bytes 2359304 | tf_op jit(solution)/shard_map/ppermute | solution.py:21
  24.9 20.1 %collective-permute-start.2 = (bf16[2,32,8,768]{3,2,1,0:T(8,128)(2,1)}, bf16[2,32,8,768]{3,2,1,0:T(8,128)(2,1)}, u32[]{:S(2)}, u32[]{:S(2)}) collective-permute-start(bf16[2,32,8,768]{3,2,1,0:T(8,128)(2,1)} %pad_maximum_fusion.5), channel_id=1, source_target_pairs={{0,1},{1,2},{2,3},{3,4},{4,5},{5,6},{6,7},{7,0},{8,9},{9,10},{10,1... | collective-permute-start | bytes 2359304 | tf_op jit(solution)/shard_map/ppermute | solution.py:20
  48.2 1.5 copy-start.6
  61.9 2.4 copy-start.3
  64.3 1.1 copy-start.2
  66.7 1.6 copy-start.5
  67.4 0.9 copy-start.1
  82.7 4.6 %copy-start.4 = (f32[8,49152]{1,0:T(8,128)S(1)}, f32[8,49152]{1,0:T(8,128)}, u32[]{:S(2)}) copy-start(f32[8,49152]{1,0:T(8,128)} %reshape_reshape.37) | copy-start | bytes 4718596
  105.7 3.2 %copy-start.9 = (bf16[2,64,12,64]{1,3,2,0:T(8,128)(2,1)S(1)}, bf16[2,64,12,64]{1,3,2,0:T(8,128)(2,1)}, u32[]{:S(2)}) copy-start(bf16[2,64,12,64]{1,3,2,0:T(8,128)(2,1)} %get-tuple-element.162) | copy-start | bytes 589828
  106.8 16.5 %collective-permute-start.5 = (bf16[2,8,24,768]{3,2,1,0:T(8,128)(2,1)}, bf16[2,8,24,768]{3,2,1,0:T(8,128)(2,1)}, u32[]{:S(2)}, u32[]{:S(2)}) collective-permute-start(bf16[2,8,24,768]{3,2,1,0:T(8,128)(2,1)} %get-tuple-element.146), channel_id=1, source_target_pairs={{8,0},{16,8},{24,16},{0,24},{9,1},{17,9},{25,17},{1,25},{10,2},{18... | collective-permute-start | bytes 1769480 | tf_op jit(solution)/shard_map/ppermute | solution.py:21
  108.3 22.6 %collective-permute-start.4 = (bf16[2,8,24,768]{3,2,1,0:T(8,128)(2,1)}, bf16[2,8,24,768]{3,2,1,0:T(8,128)(2,1)}, u32[]{:S(2)}, u32[]{:S(2)}) collective-permute-start(bf16[2,8,24,768]{3,2,1,0:T(8,128)(2,1)} %get-tuple-element.145), channel_id=1, source_target_pairs={{0,8},{8,16},{16,24},{24,0},{1,9},{9,17},{17,25},{25,1},{2,10},{10... | collective-permute-start | bytes 1769480 | tf_op jit(solution)/shard_map/ppermute | solution.py:20
  114.8 154.9 %all-reduce.5.cloned.1.call-start = ((), (), s32[]{:S(2)}) async-start(), calls=%async_computation.1 | async-start | bytes 4718592 | tf_op jit(solution)/shard_map/psum | solution.py:209
  133.7 68.9 %collective-permute-start.7 = (bf16[2,48,8,768]{3,2,1,0:T(8,128)(2,1)}, bf16[2,48,8,768]{3,2,1,0:T(8,128)(2,1)}, u32[]{:S(2)}, u32[]{:S(2)}) collective-permute-start(bf16[2,48,8,768]{3,2,1,0:T(8,128)(2,1)} %get-tuple-element.144), channel_id=1, source_target_pairs={{1,0},{2,1},{3,2},{4,3},{5,4},{6,5},{7,6},{0,7},{9,8},{10,9},{11,1... | collective-permute-start | bytes 3538952 | tf_op jit(solution)/shard_map/ppermute | solution.py:21
  137.2 65.3 %collective-permute-start.6 = (bf16[2,48,8,768]{3,2,1,0:T(8,128)(2,1)}, bf16[2,48,8,768]{3,2,1,0:T(8,128)(2,1)}, u32[]{:S(2)}, u32[]{:S(2)}) collective-permute-start(bf16[2,48,8,768]{3,2,1,0:T(8,128)(2,1)} %get-tuple-element.143), channel_id=1, source_target_pairs={{0,1},{1,2},{2,3},{3,4},{4,5},{5,6},{6,7},{7,0},{8,9},{9,10},{10,1... | collective-permute-start | bytes 3538952 | tf_op jit(solution)/shard_map/ppermute | solution.py:20
Sparse Core Ops, SparseCore 0:
  114.9 78.7 all-reduce.2
  196.9 72.8 all-reduce.4
